TPU v7x, 256 devices: a whole 4x4x8 slice. The times are simulated.
256 devices in a mesh: wafer: 4 (over y), span: 64 (over z, x, core).
Axes of the slice: x: 4, y: 4, z: 8, core: 2. Of those that a mesh axis runs over, the one named last changes fastest.
Arguments:
- timestream: float32 [1536, 16384], P(('wafer', 'span')), may hold values from -6 to 6
- templates: float32 [64, 16384], P(None, 'span'), may hold values from -0.046875 to 0.046875
- bias_group: int32 [1536], P('wafer'), may hold values from 0 to 11, as said below
- det_weight: float32 [1536], P('wafer'), may hold values from 0.2 to 5
- cut_start: int32 [1536], P('wafer'), may hold values from 0 to 16383
- cut_len: int32 [1536], P('wafer'), may hold values from 1 to 511
- pointing: int32 [1536, 16384], P('wafer', 'span'), may hold values from 0 to 32767
- hit_tiles: int32 [64, 64], replicated, may hold values from 0 to 511, as said below
Outputs:
- fit_coeffs: float32 [1536, 64], P(('wafer', 'span'))
- rhs_map: float32 [512, 512], P('span', 'wafer')
- weight_map: float32 [512, 512], P('span', 'wafer')
Inputs may be any that keep to these rules, and one draw needn't show every extreme that they name: `bias_group`: within each wafer's 384 detectors every bias line holds exactly 32 detectors. `hit_tiles`: each row lists distinct tiles; tile t is owned by index t // 8 of span; every row holds exactly 2 tiles of each owner it names: of one owner common to all rows, and of 31 other owners.
All inputs are finite; a program needn't handle non-finite values.
Results may differ from a plain program's by a relative error of at most 0.0041.
Values sent between devices are 32-bit elements; how exact they have to be, the bound alone decides.
No kernel may reach another device: no remote copies, remote signals or barrier semaphores. Data moves between devices by JAX's collectives and lax.ppermute only.
A program may use at most 64 MiB of HBM per device.

v0:
```python
import math
import jax
import jax.numpy as jnp
from jax import lax
from jax.sharding import PartitionSpec as P

NGROUP = 12
TILE = 512
TILE_OWN = 8


def solve_normal(matrix, right_side):
    factor = jnp.linalg.cholesky(matrix)
    middle = lax.linalg.triangular_solve(factor, right_side, left_side=True, lower=True)
    return lax.linalg.triangular_solve(factor, middle, left_side=True, lower=True, transpose_a=True)


def bin_samples(weighted, sample_weight, pointing, tiles_listed):
    rows = weighted.shape[0]
    block_dets = math.gcd(rows, 64)
    block_count = rows // block_dets
    fine_width = min(128, TILE)
    coarse_width = tiles_listed * TILE // fine_width
    blocks = (
        weighted.reshape(block_count, -1),
        sample_weight.reshape(block_count, -1),
        pointing.reshape(block_count, -1),
    )
    zero_value = jnp.zeros((), jnp.bfloat16)

    def accumulate(totals, block_data):
        values_block, weights_block, points_block = block_data
        coarse_index = points_block // fine_width
        fine_index = points_block % fine_width
        coarse_hot = coarse_index[None, :] == jnp.arange(coarse_width, dtype=jnp.int32)[:, None]
        left_hot = jnp.concatenate(
            [
                jnp.where(coarse_hot, values_block[None, :], zero_value),
                jnp.where(coarse_hot, weights_block[None, :], zero_value),
            ],
            axis=0,
        )
        right_hot = (
            fine_index[None, :] == jnp.arange(fine_width, dtype=jnp.int32)[:, None]
        ).astype(jnp.bfloat16)
        product = lax.dot_general(
            left_hot, right_hot, (((1,), (1,)), ((), ())), preferred_element_type=jnp.float32
        )
        return (totals + product, None)

    totals, unused = lax.scan(
        accumulate, jnp.zeros((2 * coarse_width, fine_width), jnp.float32), blocks
    )
    return totals.reshape(2, tiles_listed, TILE)


def body(timestream, templates, bias_group, det_weight, cut_start, cut_len, pointing, hit_tiles):
    highest = lax.Precision.HIGHEST
    spans = lax.axis_size("span")
    own_index = lax.axis_index("span")
    det_dev = timestream.shape[0]
    span_len = templates.shape[1]
    det_wafer = det_dev * spans
    line_scale = NGROUP / det_wafer
    groups = lax.dynamic_slice_in_dim(bias_group, own_index * det_dev, det_dev)
    onehot = (groups[None, :] == jnp.arange(NGROUP, dtype=jnp.int32)[:, None]).astype(jnp.float32)
    line_sums = lax.psum(
        jnp.dot(onehot, timestream, precision=highest, preferred_element_type=jnp.float32), "span"
    )
    cleaned = timestream - jnp.dot(
        onehot.T, line_sums * line_scale, precision=highest, preferred_element_type=jnp.float32
    )
    all_templates = lax.all_gather(templates, "span", axis=1, tiled=True)
    normal_matrix = jnp.dot(
        all_templates, all_templates.T, precision=highest, preferred_element_type=jnp.float32
    )
    projection = jnp.dot(
        all_templates, cleaned.T, precision=highest, preferred_element_type=jnp.float32
    )
    amplitudes = solve_normal(normal_matrix, projection)
    fit_coeffs = amplitudes.T
    outgoing = cleaned - jnp.dot(
        amplitudes.T, all_templates, precision=highest, preferred_element_type=jnp.float32
    )
    regrouped = lax.all_to_all(outgoing, "span", split_axis=1, concat_axis=0, tiled=True)
    sample_time = own_index * span_len + jnp.arange(span_len, dtype=jnp.int32)
    inside = (sample_time[None, :] >= cut_start[:, None]) & (
        sample_time[None, :] < (cut_start + cut_len)[:, None]
    )
    sample_weight = jnp.where(inside, jnp.float32(0.0), det_weight[:, None]).astype(jnp.bfloat16)
    weighted = (sample_weight.astype(jnp.float32) * regrouped).astype(jnp.bfloat16)
    tiles_listed = hit_tiles.shape[1]
    partial_value = bin_samples(weighted, sample_weight, pointing, tiles_listed)
    shared = lax.psum_scatter(partial_value, "wafer", scatter_dimension=2, tiled=True)
    own_tiles = lax.dynamic_index_in_dim(hit_tiles, own_index, 0, keepdims=False)
    selector = (
        own_tiles[None, :] == jnp.arange(lax.axis_size("span") * TILE_OWN, dtype=jnp.int32)[:, None]
    ).astype(jnp.float32)
    owned_tiles = lax.psum_scatter(
        jnp.einsum("rs,ksp->rkp", selector, shared, precision=highest),
        "span",
        scatter_dimension=0,
        tiled=True,
    )
    return (fit_coeffs, owned_tiles[:, 0, :], owned_tiles[:, 1, :])


def solution(mesh):
    in_specs = (
        P(("wafer", "span"), None),
        P(None, "span"),
        P("wafer"),
        P("wafer"),
        P("wafer"),
        P("wafer"),
        P("wafer", "span"),
        P(),
    )
    out_specs = (P(("wafer", "span"), None), P("span", "wafer"), P("span", "wafer"))
    return jax.shard_map(body, mesh=mesh, in_specs=in_specs, out_specs=out_specs, check_vma=False)
```

profile of v0, /device:TPU:8, one launch (start us, length us, event | category | flops | bytes accessed | tf_op | source)
XLA Modules:
  0.0 608.7 jit_solution(14513693516777914590)
XLA Ops:
  7.2 0.8 dynamic_slice.27
  8.0 2.6 fusion.23
  10.7 0.7 all-gather.2.cloned.1.call-update
  11.4 190.2 %all-reduce.2.cloned.1.call-done = f32[12,16384]{1,0:T(8,128)} async-done(((f32[12,16384]{1,0:T(8,128)}), f32[12,16384]{1,0:T(8,128)}) %all-reduce.2.cloned.1.call-update) | async-done | bytes 786448 | tf_op jit(solution)/shard_map/psum | solution.py:67
  201.5 1.9 convolution_subtract_fusion.1
  203.5 73.8 %all-gather.2.cloned.1.call-done = f32[64,16384]{1,0:T(8,128)} async-done(((f32[64,256]{1,0:T(8,128)}), f32[64,16384]{1,0:T(8,128)}) %all-gather.2.cloned.1.call-update) | async-done | bytes 4194320 | tf_op jit(solution)/shard_map/all_gather | solution.py:73
  277.3 6.9 %fusion.27 = f32[64,64]{1,0:T(8,128)S(1)} fusion(f32[64,16384]{1,0:T(8,128)} %all-gather.2.cloned.1.call-done), kind=kOutput, calls=%fused_computation.53 | convolution fusion | flops 805306368 | bytes 4210688 | tf_op jit(solution)/shard_map/dot_general | solution.py:74
  284.4 5.8 cholesky.16
  290.9 0.7 fusion.17
  291.6 4.9 custom-call.8
  296.4 5.1 fusion.28
  302.0 5.1 convolution_subtract_fusion
  307.1 8.5 %all-to-all-start = ((f32[6,64,256]{2,0,1:T(8,128)}), f32[6,64,256]{2,0,1:T(8,128)S(1)}, u32[]{:S(2)}, u32[]{:S(2)}) async-start(f32[6,64,256]{2,0,1:T(8,128)} %bitcast.6), calls=%async_computation | async-start | bytes 1048576 | tf_op jit(solution)/shard_map/all_to_all | solution.py:85
  317.3 16.0 %all-to-all-done = f32[6,64,256]{2,0,1:T(8,128)S(1)} async-done(((f32[6,64,256]{2,0,1:T(8,128)}), f32[6,64,256]{2,0,1:T(8,128)S(1)}, u32[]{:S(2)}, u32[]{:S(2)}) %all-to-all-start) | async-done | bytes 393248 | tf_op jit(solution)/shard_map/all_to_all | solution.py:85
  333.5 112.1 %while.13 = (s32[]{:T(128)}, f32[512,128]{1,0:T(8,128)S(1)}, s32[6,16384]{1,0:T(8,128)S(1)}, bf16[6,16384]{1,0:T(8,128)(2,1)S(1)}, bf16[6,16384]{1,0:T(8,128)(2,1)S(1)}, /*index=5*/s32[]{:T(128)}, s32[]{:T(128)}) while((s32[]{:T(128)}, f32[512,128]{1,0:T(8,128)S(1)}, s32[6,16384]{1,0:T(8,128)S(1)}, bf16[6,16384]{1,0:T(8,128)(2,1)S(1)}, ...), condition=%wide.region_4.5_spmd.clone, body=%wide.region_3.4_spmd.clone.sunk | while | flops 2196176896 | bytes 34734180 | solution.py:51
  334.4 9.2 %fusion.43 = (bf16[256,16384]{1,0:T(8,128)(2,1)}, bf16[256,16384]{1,0:T(8,128)(2,1)}) fusion(s32[16384]{0:T(1024)S(1)} %bitcast.51, bf16[16384]{0:T(1024)(128)(2,1)S(1)} %get-tuple-element.149, bf16[16384]{0:T(1024)(128)(2,1)S(1)} %get-tuple-element.150), kind=kLoop, calls=%fused_computation.6.clone.1 | loop fusion | flops 12582912 | bytes 16908288 | tf_op jit(solution)/shard_map/while/body/eval_jaxpr/jit(_where)/select_n | solution.py:38
  343.6 8.6 %fusion.44 = f32[512,128]{1,0:T(8,128)S(1)} fusion(s32[16384]{0:T(1024)S(1)} %bitcast.55, bf16[256,16384]{1,0:T(8,128)(2,1)} %get-tuple-element.151, bf16[256,16384]{1,0:T(8,128)(2,1)} %get-tuple-element.152, f32[512,128]{1,0:T(8,128)S(1)} %get-tuple-element.161, pred[]{:T(512)S(6)} %compare.24), kind=kOutput, calls=%fused_computation.9.clone.1 | convolution fusion | flops 2183266304 | bytes 17367040 | tf_op jit(solution)/shard_map/while/body/eval_jaxpr/dot_general | solution.py:46
  353.1 9.2 %fusion.43 = (bf16[256,16384]{1,0:T(8,128)(2,1)}, bf16[256,16384]{1,0:T(8,128)(2,1)}) fusion(s32[16384]{0:T(1024)S(1)} %bitcast.51, bf16[16384]{0:T(1024)(128)(2,1)S(1)} %get-tuple-element.149, bf16[16384]{0:T(1024)(128)(2,1)S(1)} %get-tuple-element.150), kind=kLoop, calls=%fused_computation.6.clone.1 | loop fusion | flops 12582912 | bytes 16908288 | tf_op jit(solution)/shard_map/while/body/eval_jaxpr/jit(_where)/select_n | solution.py:38
  362.3 8.6 %fusion.44 = f32[512,128]{1,0:T(8,128)S(1)} fusion(s32[16384]{0:T(1024)S(1)} %bitcast.55, bf16[256,16384]{1,0:T(8,128)(2,1)} %get-tuple-element.151, bf16[256,16384]{1,0:T(8,128)(2,1)} %get-tuple-element.152, f32[512,128]{1,0:T(8,128)S(1)} %get-tuple-element.161, pred[]{:T(512)S(6)} %compare.24), kind=kOutput, calls=%fused_computation.9.clone.1 | convolution fusion | flops 2183266304 | bytes 17367040 | tf_op jit(solution)/shard_map/while/body/eval_jaxpr/dot_general | solution.py:46
  371.8 9.2 %fusion.43 = (bf16[256,16384]{1,0:T(8,128)(2,1)}, bf16[256,16384]{1,0:T(8,128)(2,1)}) fusion(s32[16384]{0:T(1024)S(1)} %bitcast.51, bf16[16384]{0:T(1024)(128)(2,1)S(1)} %get-tuple-element.149, bf16[16384]{0:T(1024)(128)(2,1)S(1)} %get-tuple-element.150), kind=kLoop, calls=%fused_computation.6.clone.1 | loop fusion | flops 12582912 | bytes 16908288 | tf_op jit(solution)/shard_map/while/body/eval_jaxpr/jit(_where)/select_n | solution.py:38
  381.0 8.6 %fusion.44 = f32[512,128]{1,0:T(8,128)S(1)} fusion(s32[16384]{0:T(1024)S(1)} %bitcast.55, bf16[256,16384]{1,0:T(8,128)(2,1)} %get-tuple-element.151, bf16[256,16384]{1,0:T(8,128)(2,1)} %get-tuple-element.152, f32[512,128]{1,0:T(8,128)S(1)} %get-tuple-element.161, pred[]{:T(512)S(6)} %compare.24), kind=kOutput, calls=%fused_computation.9.clone.1 | convolution fusion | flops 2183266304 | bytes 17367040 | tf_op jit(solution)/shard_map/while/body/eval_jaxpr/dot_general | solution.py:46
  390.5 9.2 %fusion.43 = (bf16[256,16384]{1,0:T(8,128)(2,1)}, bf16[256,16384]{1,0:T(8,128)(2,1)}) fusion(s32[16384]{0:T(1024)S(1)} %bitcast.51, bf16[16384]{0:T(1024)(128)(2,1)S(1)} %get-tuple-element.149, bf16[16384]{0:T(1024)(128)(2,1)S(1)} %get-tuple-element.150), kind=kLoop, calls=%fused_computation.6.clone.1 | loop fusion | flops 12582912 | bytes 16908288 | tf_op jit(solution)/shard_map/while/body/eval_jaxpr/jit(_where)/select_n | solution.py:38
  399.7 8.6 %fusion.44 = f32[512,128]{1,0:T(8,128)S(1)} fusion(s32[16384]{0:T(1024)S(1)} %bitcast.55, bf16[256,16384]{1,0:T(8,128)(2,1)} %get-tuple-element.151, bf16[256,16384]{1,0:T(8,128)(2,1)} %get-tuple-element.152, f32[512,128]{1,0:T(8,128)S(1)} %get-tuple-element.161, pred[]{:T(512)S(6)} %compare.24), kind=kOutput, calls=%fused_computation.9.clone.1 | convolution fusion | flops 2183266304 | bytes 17367040 | tf_op jit(solution)/shard_map/while/body/eval_jaxpr/dot_general | solution.py:46
  409.1 9.2 %fusion.43 = (bf16[256,16384]{1,0:T(8,128)(2,1)}, bf16[256,16384]{1,0:T(8,128)(2,1)}) fusion(s32[16384]{0:T(1024)S(1)} %bitcast.51, bf16[16384]{0:T(1024)(128)(2,1)S(1)} %get-tuple-element.149, bf16[16384]{0:T(1024)(128)(2,1)S(1)} %get-tuple-element.150), kind=kLoop, calls=%fused_computation.6.clone.1 | loop fusion | flops 12582912 | bytes 16908288 | tf_op jit(solution)/shard_map/while/body/eval_jaxpr/jit(_where)/select_n | solution.py:38
  418.3 8.6 %fusion.44 = f32[512,128]{1,0:T(8,128)S(1)} fusion(s32[16384]{0:T(1024)S(1)} %bitcast.55, bf16[256,16384]{1,0:T(8,128)(2,1)} %get-tuple-element.151, bf16[256,16384]{1,0:T(8,128)(2,1)} %get-tuple-element.152, f32[512,128]{1,0:T(8,128)S(1)} %get-tuple-element.161, pred[]{:T(512)S(6)} %compare.24), kind=kOutput, calls=%fused_computation.9.clone.1 | convolution fusion | flops 2183266304 | bytes 17367040 | tf_op jit(solution)/shard_map/while/body/eval_jaxpr/dot_general | solution.py:46
  427.8 9.2 %fusion.43 = (bf16[256,16384]{1,0:T(8,128)(2,1)}, bf16[256,16384]{1,0:T(8,128)(2,1)}) fusion(s32[16384]{0:T(1024)S(1)} %bitcast.51, bf16[16384]{0:T(1024)(128)(2,1)S(1)} %get-tuple-element.149, bf16[16384]{0:T(1024)(128)(2,1)S(1)} %get-tuple-element.150), kind=kLoop, calls=%fused_computation.6.clone.1 | loop fusion | flops 12582912 | bytes 16908288 | tf_op jit(solution)/shard_map/while/body/eval_jaxpr/jit(_where)/select_n | solution.py:38
  437.0 8.6 %fusion.44 = f32[512,128]{1,0:T(8,128)S(1)} fusion(s32[16384]{0:T(1024)S(1)} %bitcast.55, bf16[256,16384]{1,0:T(8,128)(2,1)} %get-tuple-element.151, bf16[256,16384]{1,0:T(8,128)(2,1)} %get-tuple-element.152, f32[512,128]{1,0:T(8,128)S(1)} %get-tuple-element.161, pred[]{:T(512)S(6)} %compare.24), kind=kOutput, calls=%fused_computation.9.clone.1 | convolution fusion | flops 2183266304 | bytes 17367040 | tf_op jit(solution)/shard_map/while/body/eval_jaxpr/dot_general | solution.py:46
  445.7 0.7 reshape.57
  446.5 18.2 %reduce-scatter.3.cloned.1.call-done = f32[2,64,128]{2,1,0:T(8,128)} async-done(((f32[2,64,512]{2,1,0:T(8,128)}), f32[2,64,128]{2,1,0:T(8,128)}) %reduce-scatter.3.cloned.1.call-update) | async-done | bytes 65552 | tf_op jit(solution)/shard_map/reduce_scatter | solution.py:94
  464.7 2.1 fusion.14
  466.9 134.0 %reduce-scatter.5.cloned.1.call-done = f32[8,2,128]{2,0,1:T(8,128)} async-done(((f32[512,2,128]{2,0,1:T(8,128)}), f32[8,2,128]{2,0,1:T(8,128)}) %reduce-scatter.5.cloned.1.call-update) | async-done | bytes 8208 | tf_op jit(solution)/shard_map/reduce_scatter | solution.py:99
  600.9 1.3 slice_bitcast_fusion
  (61 shorter events, 8.1 us)
Async XLA Ops:
  7.2 439.3 %copy-start = (s32[64,64]{1,0:T(8,128)S(1)}, s32[64,64]{1,0:T(8,128)}, u32[]{:S(2)}) copy-start(s32[64,64]{1,0:T(8,128)} %param.17) | copy-start | bytes 49156
  7.2 194.4 %all-reduce.2.cloned.1.call-start = ((), (), s32[]{:S(2)}) async-start(), calls=%async_computation.4 | async-start | bytes 2097152 | tf_op jit(solution)/shard_map/psum | solution.py:67
  10.6 266.7 %all-gather.2.cloned.1.call-start = ((), (), s32[]{:S(2)}) async-start(), calls=%async_computation.3 | async-start | bytes 4259840 | tf_op jit(solution)/shard_map/all_gather | solution.py:73
  203.4 112.4 %copy-start.5 = (f32[384]{0:T(512)S(1)}, f32[384]{0:T(512)}, u32[]{:S(2)}) copy-start(f32[384]{0:T(512)} %param.13) | copy-start | bytes 4612
  203.4 112.5 %copy-start.3 = (s32[384]{0:T(512)S(1)}, s32[384]{0:T(512)}, u32[]{:S(2)}) copy-start(s32[384]{0:T(512)} %param.14) | copy-start | bytes 4612
  203.5 112.6 %copy-start.4 = (s32[384]{0:T(512)S(1)}, s32[384]{0:T(512)}, u32[]{:S(2)}) copy-start(s32[384]{0:T(512)} %param.15) | copy-start | bytes 4612
  284.3 32.9 %copy-start.1 = (s32[384,256]{1,0:T(8,128)S(1)}, s32[384,256]{1,0:T(8,128)}, u32[]{:S(2)}) copy-start(s32[384,256]{1,0:T(8,128)} %param.16) | copy-start | bytes 1179652
  302.0 31.6 %copy-start.2 = (f32[64,6]{0,1:T(8,128)}, f32[64,6]{0,1:T(8,128)S(1)}, u32[]{:S(2)}) copy-start(f32[64,6]{0,1:T(8,128)S(1)} %fusion.18) | copy-start | bytes 4612
  307.1 26.2 %all-to-all-start = ((f32[6,64,256]{2,0,1:T(8,128)}), f32[6,64,256]{2,0,1:T(8,128)S(1)}, u32[]{:S(2)}, u32[]{:S(2)}) async-start(f32[6,64,256]{2,0,1:T(8,128)} %bitcast.6), calls=%async_computation | async-start | bytes 1048576 | tf_op jit(solution)/shard_map/all_to_all | solution.py:85
  315.6 149.1 %reduce-scatter.3.cloned.1.call-start = ((), (), s32[]{:S(2)}) async-start(), calls=%async_computation.5 | async-start | bytes 327680 | tf_op jit(solution)/shard_map/reduce_scatter | solution.py:94
  446.5 154.4 %reduce-scatter.5.cloned.1.call-start = ((), (), s32[]{:S(2)}) async-start(), calls=%async_computation.6 | async-start | bytes 532480 | tf_op jit(solution)/shard_map/reduce_scatter | solution.py:99
Sparse Core Ops, SparseCore 0:
  11.4 190.0 all-reduce.1
  204.2 73.0 all-gather.1
  446.6 18.1 reduce-scatter.2
  468.5 132.3 reduce-scatter.4
where the time goes:
time: 609 us
  waiting for transfers between devices  433 us (71%)
  matrix products  76 us (12%)
  other arithmetic  69.9 us (11%)
  between operations  14 us (2%)
  starting transfers between devices  8.88 us (1%)
  local copies, waits for them, and re-layouts  6.68 us (1%)
    psum x1, waiting for transfers between devices, body(): lax.psum(jnp.dot(onehot, timestream, precision=highest, preferred_element...  190 us
    reduce_scatter x1, waiting for transfers between devices, body(): lax.psum_scatter(jnp.einsum('rs,ksp->rkp', selector, shared, precision=hi...  134 us
    all_gather x1, waiting for transfers between devices, body(): all_templates = lax.all_gather(templates, 'span', axis=1, tiled=True)  73.8 us
    select_n x6, other arithmetic, accumulate(): jnp.where(coarse_hot, values_block[None, :], zero_value)  55.2 us
    dot_general x6, matrix products, accumulate(): lax.dot_general(left_hot, right_hot, (((1,), (1,)), ((), ())), preferred_...  51.9 us
    reduce_scatter x1, waiting for transfers between devices, body(): lax.psum_scatter(partial_value, 'wafer', scatter_dimension=2, tiled=True)  18.2 us
    all_to_all x1, waiting for transfers between devices, body(): lax.all_to_all(outgoing, 'span', split_axis=1, concat_axis=0, tiled=True)  16 us
  transfers between devices with their start and end apart: 5, of which 5 were waited for; matrix products, arithmetic and copies ran while one was open for 1% of the time, Pallas kernels for 0%

commit v1 on v0

--- a/solution.py
+++ b/solution.py
@@ -70,7 +70,9 @@
     cleaned = timestream - jnp.dot(
         onehot.T, line_sums * line_scale, precision=highest, preferred_element_type=jnp.float32
     )
-    all_templates = lax.all_gather(templates, "span", axis=1, tiled=True)
+    all_templates = jnp.concatenate(
+        lax.all_to_all(jnp.stack([templates] * lax.axis_size("span")), "span", 0, 0), axis=1
+    )
     normal_matrix = jnp.dot(
         all_templates, all_templates.T, precision=highest, preferred_element_type=jnp.float32
     )

time: 609 us -> 564 us (0.926)
  waiting for transfers between devices: 433 us -> 377 us
  starting transfers between devices: 8.88 us -> 18.5 us
    all_gather x1 -> x0, waiting for transfers between devices: 73.8 us -> none  [body(): all_templates = lax.all_gather(templates, 'span', axis=1, tiled=True)]
    psum x1, waiting for transfers between devices: 190 us -> 209 us  [body(): lax.psum(jnp.dot(onehot, timestream, precision=highest, preferred_element...]
    all_to_all x0 -> x1, starting transfers between devices: none -> 12.2 us  [body(): lax.all_to_all(jnp.stack([templates] * lax.axis_size('span')), 'span', 0, 0)]
  transfers between devices with their start and end apart: 5 -> 5, of which waited for: 5 -> 4; matrix products, arithmetic and copies ran while one was open for 1% -> 1% of each run, Pallas kernels for 0% -> 0%
where the time goes in v1:
time: 564 us
  waiting for transfers between devices  377 us (67%)
  matrix products  71 us (13%)
  other arithmetic  69.9 us (12%)
  starting transfers between devices  18.5 us (3%)
  between operations  14 us (2%)
  local copies, waits for them, and re-layouts  12.7 us (2%)
    psum x1, waiting for transfers between devices, body(): lax.psum(jnp.dot(onehot, timestream, precision=highest, preferred_element...  209 us
    reduce_scatter x1, waiting for transfers between devices, body(): lax.psum_scatter(jnp.einsum('rs,ksp->rkp', selector, shared, precision=hi...  134 us
    select_n x6, other arithmetic, accumulate(): jnp.where(coarse_hot, values_block[None, :], zero_value)  55.2 us
    dot_general x6, matrix products, accumulate(): lax.dot_general(left_hot, right_hot, (((1,), (1,)), ((), ())), preferred_...  51.9 us
    reduce_scatter x1, waiting for transfers between devices, body(): lax.psum_scatter(partial_value, 'wafer', scatter_dimension=2, tiled=True)  18.2 us
    all_to_all x1, waiting for transfers between devices, body(): lax.all_to_all(outgoing, 'span', split_axis=1, concat_axis=0, tiled=True)  16.1 us
    all_to_all x1, starting transfers between devices, body(): lax.all_to_all(jnp.stack([templates] * lax.axis_size('span')), 'span', 0, 0)  12.2 us
  transfers between devices with their start and end apart: 5, of which 4 were waited for; matrix products, arithmetic and copies ran while one was open for 1% of the time, Pallas kernels for 0%

profile of v1, /device:TPU:8, one launch (start us, length us, event | category | flops | bytes accessed | tf_op | source)
XLA Modules:
  0.0 563.7 jit_solution(4204769760759083717)
XLA Ops:
  7.2 3.4 stack.2
  10.6 12.2 %all-to-all-start = ((f32[64,64,256]{2,1,0:T(8,128)}), f32[64,64,256]{2,1,0:T(8,128)}, u32[]{:S(2)}, u32[]{:S(2)}) async-start(f32[64,64,256]{2,1,0:T(8,128)} %stack.2), calls=%async_computation | async-start | bytes 8388608 | tf_op jit(solution)/shard_map/all_to_all | solution.py:74
  22.8 0.8 dynamic_slice.27
  23.6 1.5 fusion.28
  25.2 208.8 %all-reduce.2.cloned.1.call-done = f32[12,16384]{1,0:T(8,128)} async-done(((f32[12,16384]{1,0:T(8,128)}), f32[12,16384]{1,0:T(8,128)}) %all-reduce.2.cloned.1.call-update) | async-done | bytes 786448 | tf_op jit(solution)/shard_map/psum | solution.py:67
  233.9 1.7 convolution_subtract_fusion.1
  235.7 6.9 %fusion.13 = f32[64,64]{1,0:T(8,128)S(1)} fusion(f32[64,64,256]{2,1,0:T(8,128)} %all-to-all-done), kind=kOutput, calls=%fused_computation.22 | convolution fusion | flops 805306368 | bytes 4210688 | tf_op jit(solution)/shard_map/dot_general | solution.py:76
  242.7 5.8 %cholesky.16 = f32[64,64]{1,0:T(8,128)S(1)} custom-call(f32[64,64]{1,0:T(8,128)S(1)} %fusion.27), custom_call_target="Cholesky" | custom-call | tf_op jit(solution)/shard_map/jit(cholesky)/cholesky | solution.py:13
  249.9 4.9 custom-call.8
  254.9 2.6 copy.16
  257.5 3.3 fusion.32
  261.3 3.1 convolution_subtract_fusion
  264.4 6.2 %all-to-all-start.1 = ((f32[6,64,256]{2,0,1:T(8,128)}), f32[6,64,256]{2,0,1:T(8,128)S(1)}, u32[]{:S(2)}, u32[]{:S(2)}) async-start(f32[6,64,256]{2,0,1:T(8,128)} %bitcast.8), calls=%async_computation.1 | async-start | bytes 1048576 | tf_op jit(solution)/shard_map/all_to_all | solution.py:87
  272.0 16.1 %all-to-all-done.1 = f32[6,64,256]{2,0,1:T(8,128)S(1)} async-done(((f32[6,64,256]{2,0,1:T(8,128)}), f32[6,64,256]{2,0,1:T(8,128)S(1)}, u32[]{:S(2)}, u32[]{:S(2)}) %all-to-all-start.1) | async-done | bytes 393248 | tf_op jit(solution)/shard_map/all_to_all | solution.py:87
  288.4 112.1 %while.13 = (s32[]{:T(128)}, f32[512,128]{1,0:T(8,128)S(1)}, s32[6,16384]{1,0:T(8,128)S(1)}, bf16[6,16384]{1,0:T(8,128)(2,1)S(1)}, bf16[6,16384]{1,0:T(8,128)(2,1)S(1)}, /*index=5*/s32[]{:T(128)}, s32[]{:T(128)}) while((s32[]{:T(128)}, f32[512,128]{1,0:T(8,128)S(1)}, s32[6,16384]{1,0:T(8,128)S(1)}, bf16[6,16384]{1,0:T(8,128)(2,1)S(1)}, ...), condition=%wide.region_4.5_spmd.clone, body=%wide.region_3.4_spmd.clone.sunk | while | flops 2196176896 | bytes 34734180 | solution.py:51
  289.3 9.2 %fusion.45 = (bf16[256,16384]{1,0:T(8,128)(2,1)}, bf16[256,16384]{1,0:T(8,128)(2,1)}) fusion(s32[16384]{0:T(1024)S(1)} %bitcast.60, bf16[16384]{0:T(1024)(128)(2,1)S(1)} %get-tuple-element.149, bf16[16384]{0:T(1024)(128)(2,1)S(1)} %get-tuple-element.150), kind=kLoop, calls=%fused_computation.6.clone.1 | loop fusion | flops 12582912 | bytes 16908288 | tf_op jit(solution)/shard_map/while/body/eval_jaxpr/jit(_where)/select_n | solution.py:38
  298.5 8.6 %fusion.46 = f32[512,128]{1,0:T(8,128)S(1)} fusion(s32[16384]{0:T(1024)S(1)} %bitcast.64, bf16[256,16384]{1,0:T(8,128)(2,1)} %get-tuple-element.151, bf16[256,16384]{1,0:T(8,128)(2,1)} %get-tuple-element.152, f32[512,128]{1,0:T(8,128)S(1)} %get-tuple-element.161, pred[]{:T(512)S(6)} %compare.24), kind=kOutput, calls=%fused_computation.9.clone.1 | convolution fusion | flops 2183266304 | bytes 17367040 | tf_op jit(solution)/shard_map/while/body/eval_jaxpr/dot_general | solution.py:46
  308.0 9.2 %fusion.45 = (bf16[256,16384]{1,0:T(8,128)(2,1)}, bf16[256,16384]{1,0:T(8,128)(2,1)}) fusion(s32[16384]{0:T(1024)S(1)} %bitcast.60, bf16[16384]{0:T(1024)(128)(2,1)S(1)} %get-tuple-element.149, bf16[16384]{0:T(1024)(128)(2,1)S(1)} %get-tuple-element.150), kind=kLoop, calls=%fused_computation.6.clone.1 | loop fusion | flops 12582912 | bytes 16908288 | tf_op jit(solution)/shard_map/while/body/eval_jaxpr/jit(_where)/select_n | solution.py:38
  317.2 8.6 %fusion.46 = f32[512,128]{1,0:T(8,128)S(1)} fusion(s32[16384]{0:T(1024)S(1)} %bitcast.64, bf16[256,16384]{1,0:T(8,128)(2,1)} %get-tuple-element.151, bf16[256,16384]{1,0:T(8,128)(2,1)} %get-tuple-element.152, f32[512,128]{1,0:T(8,128)S(1)} %get-tuple-element.161, pred[]{:T(512)S(6)} %compare.24), kind=kOutput, calls=%fused_computation.9.clone.1 | convolution fusion | flops 2183266304 | bytes 17367040 | tf_op jit(solution)/shard_map/while/body/eval_jaxpr/dot_general | solution.py:46
  326.7 9.2 %fusion.45 = (bf16[256,16384]{1,0:T(8,128)(2,1)}, bf16[256,16384]{1,0:T(8,128)(2,1)}) fusion(s32[16384]{0:T(1024)S(1)} %bitcast.60, bf16[16384]{0:T(1024)(128)(2,1)S(1)} %get-tuple-element.149, bf16[16384]{0:T(1024)(128)(2,1)S(1)} %get-tuple-element.150), kind=kLoop, calls=%fused_computation.6.clone.1 | loop fusion | flops 12582912 | bytes 16908288 | tf_op jit(solution)/shard_map/while/body/eval_jaxpr/jit(_where)/select_n | solution.py:38
  335.9 8.6 %fusion.46 = f32[512,128]{1,0:T(8,128)S(1)} fusion(s32[16384]{0:T(1024)S(1)} %bitcast.64, bf16[256,16384]{1,0:T(8,128)(2,1)} %get-tuple-element.151, bf16[256,16384]{1,0:T(8,128)(2,1)} %get-tuple-element.152, f32[512,128]{1,0:T(8,128)S(1)} %get-tuple-element.161, pred[]{:T(512)S(6)} %compare.24), kind=kOutput, calls=%fused_computation.9.clone.1 | convolution fusion | flops 2183266304 | bytes 17367040 | tf_op jit(solution)/shard_map/while/body/eval_jaxpr/dot_general | solution.py:46
  345.4 9.2 %fusion.45 = (bf16[256,16384]{1,0:T(8,128)(2,1)}, bf16[256,16384]{1,0:T(8,128)(2,1)}) fusion(s32[16384]{0:T(1024)S(1)} %bitcast.60, bf16[16384]{0:T(1024)(128)(2,1)S(1)} %get-tuple-element.149, bf16[16384]{0:T(1024)(128)(2,1)S(1)} %get-tuple-element.150), kind=kLoop, calls=%fused_computation.6.clone.1 | loop fusion | flops 12582912 | bytes 16908288 | tf_op jit(solution)/shard_map/while/body/eval_jaxpr/jit(_where)/select_n | solution.py:38
  354.6 8.6 %fusion.46 = f32[512,128]{1,0:T(8,128)S(1)} fusion(s32[16384]{0:T(1024)S(1)} %bitcast.64, bf16[256,16384]{1,0:T(8,128)(2,1)} %get-tuple-element.151, bf16[256,16384]{1,0:T(8,128)(2,1)} %get-tuple-element.152, f32[512,128]{1,0:T(8,128)S(1)} %get-tuple-element.161, pred[]{:T(512)S(6)} %compare.24), kind=kOutput, calls=%fused_computation.9.clone.1 | convolution fusion | flops 2183266304 | bytes 17367040 | tf_op jit(solution)/shard_map/while/body/eval_jaxpr/dot_general | solution.py:46
  364.0 9.2 %fusion.45 = (bf16[256,16384]{1,0:T(8,128)(2,1)}, bf16[256,16384]{1,0:T(8,128)(2,1)}) fusion(s32[16384]{0:T(1024)S(1)} %bitcast.60, bf16[16384]{0:T(1024)(128)(2,1)S(1)} %get-tuple-element.149, bf16[16384]{0:T(1024)(128)(2,1)S(1)} %get-tuple-element.150), kind=kLoop, calls=%fused_computation.6.clone.1 | loop fusion | flops 12582912 | bytes 16908288 | tf_op jit(solution)/shard_map/while/body/eval_jaxpr/jit(_where)/select_n | solution.py:38
  373.2 8.6 %fusion.46 = f32[512,128]{1,0:T(8,128)S(1)} fusion(s32[16384]{0:T(1024)S(1)} %bitcast.64, bf16[256,16384]{1,0:T(8,128)(2,1)} %get-tuple-element.151, bf16[256,16384]{1,0:T(8,128)(2,1)} %get-tuple-element.152, f32[512,128]{1,0:T(8,128)S(1)} %get-tuple-element.161, pred[]{:T(512)S(6)} %compare.24), kind=kOutput, calls=%fused_computation.9.clone.1 | convolution fusion | flops 2183266304 | bytes 17367040 | tf_op jit(solution)/shard_map/while/body/eval_jaxpr/dot_general | solution.py:46
  382.7 9.2 %fusion.45 = (bf16[256,16384]{1,0:T(8,128)(2,1)}, bf16[256,16384]{1,0:T(8,128)(2,1)}) fusion(s32[16384]{0:T(1024)S(1)} %bitcast.60, bf16[16384]{0:T(1024)(128)(2,1)S(1)} %get-tuple-element.149, bf16[16384]{0:T(1024)(128)(2,1)S(1)} %get-tuple-element.150), kind=kLoop, calls=%fused_computation.6.clone.1 | loop fusion | flops 12582912 | bytes 16908288 | tf_op jit(solution)/shard_map/while/body/eval_jaxpr/jit(_where)/select_n | solution.py:38
  391.9 8.6 %fusion.46 = f32[512,128]{1,0:T(8,128)S(1)} fusion(s32[16384]{0:T(1024)S(1)} %bitcast.64, bf16[256,16384]{1,0:T(8,128)(2,1)} %get-tuple-element.151, bf16[256,16384]{1,0:T(8,128)(2,1)} %get-tuple-element.152, f32[512,128]{1,0:T(8,128)S(1)} %get-tuple-element.161, pred[]{:T(512)S(6)} %compare.24), kind=kOutput, calls=%fused_computation.9.clone.1 | convolution fusion | flops 2183266304 | bytes 17367040 | tf_op jit(solution)/shard_map/while/body/eval_jaxpr/dot_general | solution.py:46
  400.6 0.7 reshape.67
  401.4 18.2 %reduce-scatter.3.cloned.1.call-done = f32[2,64,128]{2,1,0:T(8,128)} async-done(((f32[2,64,512]{2,1,0:T(8,128)}), f32[2,64,128]{2,1,0:T(8,128)}) %reduce-scatter.3.cloned.1.call-update) | async-done | bytes 65552 | tf_op jit(solution)/shard_map/reduce_scatter | solution.py:96
  419.7 2.1 fusion.19
  421.8 134.1 %reduce-scatter.5.cloned.1.call-done = f32[8,2,128]{2,0,1:T(8,128)} async-done(((f32[512,2,128]{2,0,1:T(8,128)}), f32[8,2,128]{2,0,1:T(8,128)}) %reduce-scatter.5.cloned.1.call-update) | async-done | bytes 8208 | tf_op jit(solution)/shard_map/reduce_scatter | solution.py:101
  555.9 1.3 slice_bitcast_fusion
  (64 shorter events, 8.6 us)
Async XLA Ops:
  7.2 394.2 %copy-start = (s32[64,64]{1,0:T(8,128)S(1)}, s32[64,64]{1,0:T(8,128)}, u32[]{:S(2)}) copy-start(s32[64,64]{1,0:T(8,128)} %param.17) | copy-start | bytes 49156
  7.2 16.4 %copy-start.1 = (f32[6,16384]{1,0:T(8,128)S(1)}, f32[6,16384]{1,0:T(8,128)}, u32[]{:S(2)}) copy-start(f32[6,16384]{1,0:T(8,128)} %param.10) | copy-start | bytes 1179652
  10.6 225.1 %all-to-all-start = ((f32[64,64,256]{2,1,0:T(8,128)}), f32[64,64,256]{2,1,0:T(8,128)}, u32[]{:S(2)}, u32[]{:S(2)}) async-start(f32[64,64,256]{2,1,0:T(8,128)} %stack.2), calls=%async_computation | async-start | bytes 8388608 | tf_op jit(solution)/shard_map/all_to_all | solution.py:74
  22.8 211.2 %all-reduce.2.cloned.1.call-start = ((), (), s32[]{:S(2)}) async-start(), calls=%async_computation.4 | async-start | bytes 2097152 | tf_op jit(solution)/shard_map/psum | solution.py:67
  254.8 15.8 %copy-start.6 = (f32[384]{0:T(512)S(1)}, f32[384]{0:T(512)}, u32[]{:S(2)}) copy-start(f32[384]{0:T(512)} %param.13) | copy-start | bytes 4612
  254.8 15.8 %copy-start.4 = (s32[384]{0:T(512)S(1)}, s32[384]{0:T(512)}, u32[]{:S(2)}) copy-start(s32[384]{0:T(512)} %param.14) | copy-start | bytes 4612
  254.9 15.9 %copy-start.5 = (s32[384]{0:T(512)S(1)}, s32[384]{0:T(512)}, u32[]{:S(2)}) copy-start(s32[384]{0:T(512)} %param.15) | copy-start | bytes 4612
  257.5 14.4 %copy-start.2 = (s32[384,256]{1,0:T(8,128)S(1)}, s32[384,256]{1,0:T(8,128)}, u32[]{:S(2)}) copy-start(s32[384,256]{1,0:T(8,128)} %param.16) | copy-start | bytes 1179652
  261.3 27.1 %copy-start.3 = (f32[64,6]{0,1:T(8,128)}, f32[64,6]{0,1:T(8,128)S(1)}, u32[]{:S(2)}) copy-start(f32[64,6]{0,1:T(8,128)S(1)} %fusion.23) | copy-start | bytes 4612
  264.4 23.8 %all-to-all-start.1 = ((f32[6,64,256]{2,0,1:T(8,128)}), f32[6,64,256]{2,0,1:T(8,128)S(1)}, u32[]{:S(2)}, u32[]{:S(2)}) async-start(f32[6,64,256]{2,0,1:T(8,128)} %bitcast.8), calls=%async_computation.1 | async-start | bytes 1048576 | tf_op jit(solution)/shard_map/all_to_all | solution.py:87
  270.5 149.1 %reduce-scatter.3.cloned.1.call-start = ((), (), s32[]{:S(2)}) async-start(), calls=%async_computation.5 | async-start | bytes 327680 | tf_op jit(solution)/shard_map/reduce_scatter | solution.py:96
  401.4 154.6 %reduce-scatter.5.cloned.1.call-start = ((), (), s32[]{:S(2)}) async-start(), calls=%async_computation.6 | async-start | bytes 532480 | tf_op jit(solution)/shard_map/reduce_scatter | solution.py:101
Sparse Core Ops, SparseCore 0:
  27.0 206.8 all-reduce.1
  401.5 18.1 reduce-scatter.2
  423.5 132.3 reduce-scatter.4
